TPU v7x, 256 devices: a whole 4x4x8 slice. The times are simulated.
256 devices in a mesh: rows: 4 (over z_hi, core), cols: 64 (over y, z_lo, x).
Axes of the slice: x: 4, y: 4, z: 8 (z_hi: 2, z_lo: 4; z = z_hi * 4 + z_lo), core: 2. Of those that a mesh axis runs over, the one named last changes fastest.
Arguments:
- weight: float32 [26624, 16384], P('rows', 'cols'), may hold values from -6 to 6
- sign_bits: int32 [16384], P('cols'), may hold values from 0 to 1
Outputs:
- rotated: bfloat16 [26624, 16384], P(('rows', 'cols'))
- column_peak: float32 [16384], P('cols')
Inputs may be any that keep to these rules, and one draw needn't show every extreme that they name: Input column m is flipped in sign where sign_bits[m] is 0.
All inputs are finite; a program needn't handle non-finite values.
Results may differ from a plain program's by a relative error of at most 0.001.
Values sent between devices are 32-bit elements; how exact they have to be, the bound alone decides.
A program may use at most 64 MiB of HBM per device.

v0:
```python
import math

import jax
import jax.numpy as jnp
from jax import lax
from jax.sharding import PartitionSpec as P


def sylvester(order):
    index = jnp.arange(order, dtype=jnp.int32)
    common = jnp.bitwise_and(index[:, None], index[None, :])
    parity = jnp.zeros((order, order), jnp.int32)
    for place in range(max(order.bit_length() - 1, 1)):
        parity = jnp.bitwise_xor(parity, jnp.bitwise_and(jnp.right_shift(common, place), 1))
    return (1 - 2 * parity).astype(jnp.float32)


def body(weight, sign_bits):
    local = weight.shape[1]
    groups = lax.axis_size("cols")
    width = local * groups
    factor = 1.0 / math.sqrt(width)
    sign = (2 * sign_bits - 1).astype(jnp.float32)
    flipped = weight * sign[None, :]
    inner_table = sylvester(local)
    outer_table = sylvester(groups)
    row_count = flipped.shape[0] // groups
    stacked = flipped.reshape(groups, row_count, local)
    piece = lax.all_to_all(stacked, "cols", split_axis=0, concat_axis=0, tiled=True)
    count = piece.shape[1]
    inner = jnp.einsum("dak,kj->daj", piece, inner_table, precision=lax.Precision.HIGHEST)
    outer = jnp.einsum("daj,de->aej", inner, outer_table, precision=lax.Precision.HIGHEST)
    exact = outer.reshape(count, width) * jnp.float32(factor)
    peaks = lax.pmax(jnp.max(jnp.abs(exact), axis=0), ("rows", "cols"))
    start = lax.axis_index("cols") * local
    column_peak = lax.dynamic_slice_in_dim(peaks, start, local, 0)
    return (exact.astype(jnp.bfloat16), column_peak)


def solution(mesh):
    placed = (P("rows", "cols"), P("cols"))
    return jax.shard_map(
        body,
        mesh=mesh,
        in_specs=placed,
        out_specs=(P(("rows", "cols"), None), P("cols")),
        check_vma=False,
    )
```

profile of v0, /device:TPU:1, one launch (start us, length us, event | category | flops | bytes accessed | tf_op | source)
XLA Modules:
  0.0 438.3 jit_solution(14936904904434796295)
XLA Ops:
  7.2 0.0 all-reduce.2.cloned.1.call-start
  7.2 0.7 add_convert_fusion
  7.9 3.4 broadcast_multiply_fusion
  11.3 164.7 %all_to_all.5 = f32[64,104,256]{2,1,0:T(8,128)S(1)} all-to-all(f32[64,104,256]{2,1,0:T(8,128)S(1)} %bitcast.15), channel_id=1, replica_groups=mesh['rows'=4,'cols'=64] {'cols'}, dimensions={0} | all-to-all | bytes 13631488 | tf_op jit(solution)/shard_map/all_to_all | solution.py:29
  176.0 7.1 %fusion = f32[64,104,256]{2,0,1:T(8,128)S(1)} fusion(f32[64,104,256]{2,1,0:T(8,128)S(1)} %all_to_all.5), kind=kOutput, calls=%fused_computation | convolution fusion | flops 5236260864 | bytes 13631488 | tf_op jit(solution)/shard_map/dak,kj->daj/dot_general | solution.py:31
  183.1 6.9 %abs_reduce_fusion = (f32[64,256]{1,0:T(8,128)S(1)}, bf16[64,104,256]{2,0,1:T(8,128)(2,1)S(1)}) fusion(f32[64,104,256]{2,0,1:T(8,128)S(1)} %fusion), kind=kOutput, calls=%fused_computation.2 | convolution fusion | flops 1315508224 | bytes 10289152 | tf_op jit(solution)/shard_map/daj,de->aej/dot_general | solution.py:32
  190.0 0.7 copy.6
  190.6 0.0 all-reduce.2.cloned.1.call-update
  190.7 4.0 copy.5
  194.7 235.4 %all-reduce.2.cloned.1.call-done = f32[16384]{0:T(1024)} async-done(((f32[16384]{0:T(1024)}), f32[16384]{0:T(1024)}) %all-reduce.2.cloned.1.call-update) | async-done | bytes 65552 | tf_op jit(solution)/shard_map/pmax | solution.py:34
  430.1 1.3 dynamic_slice.3
Async XLA Ops:
  7.2 422.9 %all-reduce.2.cloned.1.call-start = ((), (), s32[]{:S(2)}) async-start(), calls=%async_computation.1 | async-start | bytes 131072 | tf_op jit(solution)/shard_map/pmax | solution.py:34
Sparse Core Ops, SparseCore 0:
  190.8 239.2 all-reduce.1
where the time goes:
time: 438 us
  waiting for transfers between devices  235 us (54%)
  blocking collectives  165 us (38%)
  between operations  14.1 us (3%)
  matrix products  14 us (3%)
  local copies, waits for them, and re-layouts  5.97 us (1%)
    pmax x1, waiting for transfers between devices, body(): peaks = lax.pmax(jnp.max(jnp.abs(exact), axis=0), ('rows', 'cols'))  235 us
    all_to_all x1, blocking collectives, body(): lax.all_to_all(stacked, 'cols', split_axis=0, concat_axis=0, tiled=True)  165 us
  transfers between devices with their start and end apart: 1, of which 1 were waited for; matrix products, arithmetic and copies ran while one was open for 1% of the time, Pallas kernels for 0%

commit v1 on v0

v1 whole, which is shorter than its diff:
```python
import functools

import jax
import jax.numpy as jnp
from jax import lax
from jax.experimental import pallas as pl
from jax.experimental.pallas import tpu as pltpu
from jax.sharding import PartitionSpec as P

MESH = pl.DeviceIdType.MESH
BLOCK = 16
TILE = 256


def sylvester(order, scale):
    row = lax.broadcasted_iota(jnp.int32, (order, order), 0)
    column = lax.broadcasted_iota(jnp.int32, (order, order), 1)
    parity = row & column
    shift = order.bit_length() // 2
    while shift:
        parity = parity ^ (parity >> shift)
        shift //= 2
    return ((1 - 2 * (parity & 1)).astype(jnp.float32) * scale).astype(jnp.bfloat16)


def butterfly(values):
    values, step = list(values), 1
    while step < len(values):
        for start in range(0, len(values), 2 * step):
            for k in range(start, start + step):
                a, b = values[k], values[k + step]
                values[k], values[k + step] = a + b, a - b
        step *= 2
    return values


def kernel(
    n, n_rows, chunks, scale,
    w_ref, bits_ref, out_ref, peak_ref,
    recv, signs, work, table, staged, peaks, row_peaks, col_in, own, row_in,
    send_sem, recv_sem, local_sem, out_sem, peak_sem,
):
    me = lax.axis_index("cols")
    my_row = lax.axis_index("rows")
    total, local = recv.shape[1], recv.shape[2]

    def peer_of(s):
        z, x, y = s & 3, (s >> 2) & 3, s >> 4
        return me ^ (y * 16 + z * 4 + x)

    mine = pltpu.make_async_copy(
        w_ref.at[pl.ds(pl.multiple_of(me * total, 8), total)], recv.at[me], local_sem.at[0]
    )
    mine.start()
    my_bits = pltpu.make_async_copy(bits_ref, signs.at[me], local_sem.at[1])
    my_bits.start()

    barrier = pltpu.get_barrier_semaphore()

    def greet(s, carry):
        pl.semaphore_signal(
            barrier, inc=1, device_id={"cols": lax.rem(me + s, n)}, device_id_type=MESH
        )
        return carry

    lax.fori_loop(1, n, greet, 0)
    for r in range(1, n_rows):
        pl.semaphore_signal(
            barrier, inc=1, device_id={"rows": lax.rem(my_row + r, n_rows)}, device_id_type=MESH
        )
    table[...] = sylvester(local, scale)
    peaks[...] = jnp.zeros_like(peaks)
    pl.semaphore_wait(barrier, n - 1 + n_rows - 1)

    count = len(chunks)
    starts = [sum(chunks[:c]) for c in range(count)]

    def send_bits(s, carry):
        pltpu.make_async_remote_copy(
            src_ref=bits_ref, dst_ref=signs.at[me],
            send_sem=send_sem.at[count], recv_sem=recv_sem.at[count],
            device_id={"cols": peer_of(s)}, device_id_type=MESH,
        ).start()
        return carry

    lax.fori_loop(1, n, send_bits, 0)

    def send_chunk(c):
        def send(s, carry):
            p = peer_of(s)
            pltpu.make_async_remote_copy(
                src_ref=w_ref.at[pl.ds(pl.multiple_of(p * total + starts[c], 8), chunks[c])],
                dst_ref=recv.at[me, pl.ds(starts[c], chunks[c])],
                send_sem=send_sem.at[c], recv_sem=recv_sem.at[c],
                device_id={"cols": p}, device_id_type=MESH,
            ).start()
            return carry

        lax.fori_loop(1, n, send, 0)

    def wait_bytes(ref, sem):
        pltpu.make_async_copy(ref, ref, sem).wait()

    for c in range(min(2, count)):
        send_chunk(c)
    mine.wait()
    my_bits.wait()
    wait_bytes(signs.at[pl.ds(0, n - 1)], recv_sem.at[count])

    for c in range(count):
        if c + 2 < count:
            send_chunk(c + 2)
        r, r0, slot = chunks[c], starts[c], c % 2
        wait_bytes(recv.at[pl.ds(0, n - 1), pl.ds(r0, r)], recv_sem.at[c])

        def inner(a, carry):
            xs = []
            for b in range(8):
                d = a * 8 + b
                sign = (2 * signs[d] - 1).astype(jnp.float32)
                xs.append(recv[d, r0:r0 + r, :] * sign)
            for b, x in enumerate(butterfly(xs)):
                work[pl.ds(pl.multiple_of((a * 8 + b) * r, 8), r), :] = x
            return carry

        lax.fori_loop(0, n // 8, inner, 0)

        def outer(b, carry):
            at = [pl.ds(pl.multiple_of((a * 8 + b) * r, 8), r) for a in range(n // 8)]
            for where, z in zip(at, butterfly([work[where, :] for where in at])):
                work[where, :] = z
            return carry

        lax.fori_loop(0, 8, outer, 0)

        if c >= 2:
            wait_bytes(staged.at[slot, pl.ds(0, chunks[c - 2])], out_sem.at[slot])

        def product(m, carry):
            z = work[pl.ds(pl.multiple_of(m * TILE, TILE), TILE), :]
            high = z.astype(jnp.bfloat16)
            low = (z - high.astype(jnp.float32)).astype(jnp.bfloat16)
            y = jnp.dot(high, table[...], preferred_element_type=jnp.float32)
            y += jnp.dot(low, table[...], preferred_element_type=jnp.float32)
            for k in range(TILE // r):
                e = m * (TILE // r) + k
                block = y[k * r:(k + 1) * r, :]
                staged[slot, 0:r, pl.ds(pl.multiple_of(e * local, local), local)] = block.astype(jnp.bfloat16)
                size = jnp.abs(block)
                top = size[0:8]
                for q in range(1, r // 8):
                    top = jnp.maximum(top, size[8 * q:8 * q + 8])
                peaks[e] = jnp.maximum(peaks[e], top)
            return carry

        lax.fori_loop(0, n * r // TILE, product, 0)
        pltpu.make_async_copy(
            staged.at[slot, pl.ds(0, r)], out_ref.at[pl.ds(r0, r)], out_sem.at[slot]
        ).start()

    def shrink(e, carry):
        row_peaks[e] = jnp.max(peaks[e], axis=0, keepdims=True)
        return carry

    lax.fori_loop(0, n, shrink, 0)

    def send_peaks(s, carry):
        p = peer_of(s)
        pltpu.make_async_remote_copy(
            src_ref=row_peaks.at[p], dst_ref=col_in.at[me],
            send_sem=peak_sem.at[0], recv_sem=peak_sem.at[1],
            device_id={"cols": p}, device_id_type=MESH,
        ).start()
        return carry

    lax.fori_loop(1, n, send_peaks, 0)
    top = row_peaks[me]
    wait_bytes(col_in.at[pl.ds(0, n - 1)], peak_sem.at[1])
    col_in[me] = top
    top = jnp.max(col_in[...], axis=0)
    own[...] = top
    for r in range(1, n_rows):
        pltpu.make_async_remote_copy(
            src_ref=own, dst_ref=row_in.at[my_row],
            send_sem=peak_sem.at[2], recv_sem=peak_sem.at[3],
            device_id={"rows": lax.rem(my_row + r, n_rows)}, device_id_type=MESH,
        ).start()
    wait_bytes(row_in.at[pl.ds(0, n_rows - 1)], peak_sem.at[3])
    row_in[my_row] = top
    peak_ref[...] = jnp.max(row_in[...], axis=0)

    wait_bytes(row_peaks.at[pl.ds(0, n - 1)], peak_sem.at[0])
    wait_bytes(row_in.at[pl.ds(0, n_rows - 1)], peak_sem.at[2])
    wait_bytes(signs.at[pl.ds(0, n - 1)], send_sem.at[count])
    for c in range(count):
        wait_bytes(recv.at[pl.ds(0, n - 1), pl.ds(starts[c], chunks[c])], send_sem.at[c])
    for c in range(max(0, count - 2), count):
        wait_bytes(staged.at[c % 2, pl.ds(0, chunks[c])], out_sem.at[c % 2])


def body(weight, sign_bits):
    rows, local = weight.shape
    n, n_rows = lax.axis_size("cols"), lax.axis_size("rows")
    total, width = rows // n, local * n
    chunks = [BLOCK] * (total // BLOCK) + ([total % BLOCK] if total % BLOCK else [])
    out, peak = pl.pallas_call(
        functools.partial(kernel, n, n_rows, chunks, width ** -0.5),
        out_shape=(
            jax.ShapeDtypeStruct((total, width), jnp.bfloat16),
            jax.ShapeDtypeStruct((1, local), jnp.float32),
        ),
        in_specs=[pl.BlockSpec(memory_space=pl.ANY)] * 2,
        out_specs=(pl.BlockSpec(memory_space=pl.ANY), pl.BlockSpec(memory_space=pltpu.VMEM)),
        scratch_shapes=[
            pltpu.VMEM((n, total, local), jnp.float32),
            pltpu.VMEM((n, 1, local), jnp.int32),
            pltpu.VMEM((n * BLOCK, local), jnp.float32),
            pltpu.VMEM((local, local), jnp.bfloat16),
            pltpu.VMEM((2, BLOCK, width), jnp.bfloat16),
            pltpu.VMEM((n, 8, local), jnp.float32),
            pltpu.VMEM((n, 1, local), jnp.float32),
            pltpu.VMEM((n, 1, local), jnp.float32),
            pltpu.VMEM((1, local), jnp.float32),
            pltpu.VMEM((n_rows, 1, local), jnp.float32),
            pltpu.SemaphoreType.DMA((len(chunks) + 1,)),
            pltpu.SemaphoreType.DMA((len(chunks) + 1,)),
            pltpu.SemaphoreType.DMA((2,)),
            pltpu.SemaphoreType.DMA((2,)),
            pltpu.SemaphoreType.DMA((4,)),
        ],
        compiler_params=pltpu.CompilerParams(collective_id=0, has_side_effects=True),
        name="rotate",
    )(weight, sign_bits.reshape(1, local))
    return out, peak.reshape(local)


def solution(mesh):
    return jax.shard_map(
        body,
        mesh=mesh,
        in_specs=(P("rows", "cols"), P("cols")),
        out_specs=(P(("rows", "cols"), None), P("cols")),
        check_vma=False,
    )
```

time: 438 us -> 184 us (0.42)
  waiting for transfers between devices: 235 us -> 0 us
  Pallas kernels: 0 us -> 179 us
  blocking collectives: 165 us -> 0 us
  matrix products: 14 us -> 0 us
  between operations: 14.1 us -> 0.65 us
    pmax x1 -> x0, waiting for transfers between devices: 235 us -> none  [body(): peaks = lax.pmax(jnp.max(jnp.abs(exact), axis=0), ('rows', 'cols'))]
    pallas_call x0 -> x1, Pallas kernels: none -> 179 us  [body(): pl.pallas_call(functools.partial(kernel, n, n_rows, chunks, width ** (-0....]
    all_to_all x1 -> x0, blocking collectives: 165 us -> none  [body(): lax.all_to_all(stacked, 'cols', split_axis=0, concat_axis=0, tiled=True)]
    dot_general x2 -> x0, matrix products: 14 us -> none  [the longest x1 7.08 us: body(): jnp.einsum('dak,kj->daj', piece, inner_table, precision=lax.Precision.HIG...]
  transfers between devices with their start and end apart: 1 -> 0, of which waited for: 1 -> 0; matrix products, arithmetic and copies ran while one was open for 1% -> 0% of each run, Pallas kernels for 0% -> 0%
where the time goes in v1:
time: 184 us
  Pallas kernels  179 us (97%)
  local copies, waits for them, and re-layouts  4.5 us (2%)
    pallas_call x1, Pallas kernels, body(): pl.pallas_call(functools.partial(kernel, n, n_rows, chunks, width ** (-0....  179 us
    unnamed x4, local copies, waits for them, and re-layouts  4.5 us

profile of v1, /device:TPU:1, one launch (start us, length us, event | category | flops | bytes accessed | tf_op | source)
XLA Modules:
  0.0 184.0 jit_solution(1701957966986773020)
XLA Ops:
  0.6 178.8 %rotate.1 = (bf16[104,16384]{1,0:T(8,128)(2,1)}, f32[1,256]{1,0:T(1,128)}) custom-call(f32[6656,256]{1,0:T(8,128)} %w_ref.1, s32[1,256]{1,0:T(1,128)} %bitcast.2), custom_call_target="tpu_custom_call" | custom-call | tf_op jit(solution)/shard_map/rotate/pallas_call | solution.py:206
  179.4 0.0 copy-start
  179.5 3.9 %copy.6 = bf16[104,16384]{1,0:T(8,128)(2,1)} copy(bf16[104,16384]{1,0:T(8,128)(2,1)} %get-tuple-element.8) | data formatting | bytes 6815744
  183.4 0.0 copy-done
  183.4 0.6 copy.7
Async XLA Ops:
  179.4 3.9 %copy-start = (f32[1,256]{1,0:T(1,128)S(1)}, f32[1,256]{1,0:T(1,128)}, u32[]{:S(2)}) copy-start(f32[1,256]{1,0:T(1,128)} %get-tuple-element.5) | copy-start | bytes 3076

commit v2 on v1

v2 whole, which is shorter than its diff:
```python
import functools

import jax
import jax.numpy as jnp
from jax import lax
from jax.experimental import pallas as pl
from jax.experimental.pallas import tpu as pltpu
from jax.sharding import PartitionSpec as P

MESH = pl.DeviceIdType.MESH
BLOCK = 16
TILE = 256
AHEAD = 2
SIDE = 4


def sylvester(order, scale):
    row = lax.broadcasted_iota(jnp.int32, (order, order), 0)
    column = lax.broadcasted_iota(jnp.int32, (order, order), 1)
    parity = row & column
    shift = order.bit_length() // 2
    while shift:
        parity = parity ^ (parity >> shift)
        shift //= 2
    return ((1 - 2 * (parity & 1)).astype(jnp.float32) * scale).astype(jnp.bfloat16)


def butterfly(values):
    values, step = list(values), 1
    while step < len(values):
        for start in range(0, len(values), 2 * step):
            for k in range(start, start + step):
                a, b = values[k], values[k + step]
                values[k], values[k + step] = a + b, a - b
        step *= 2
    return values


def kernel(
    n, n_rows, chunks, scale,
    w_ref, bits_ref, out_ref, peak_ref,
    recv, signs, work, table, peaks, row_peaks, peak_in, own, core_in,
    send_sem, recv_sem, local_sem, sign_send, sign_recv, peak_sem, hello,
):
    me = lax.axis_index("cols")
    my_row = lax.axis_index("rows")
    total, local = recv.shape[1], recv.shape[2]
    count = len(chunks)
    starts = [sum(chunks[:c]) for c in range(count)]
    y, z, x = me // 16, (me // 4) % 4, me % 4
    spot = y * 16 + x * 4 + z

    def at(yy, zz, xx):
        return yy * 16 + zz * 4 + xx

    def peer_of(s):
        zz, xx, yy = s & 3, (s >> 2) & 3, s >> 4
        return me ^ at(yy, zz, xx)

    def wait_bytes(ref, sem):
        pltpu.make_async_copy(ref, ref, sem).wait()

    mine = pltpu.make_async_copy(
        w_ref.at[pl.ds(pl.multiple_of(me * total, 8), total)], recv.at[me], local_sem.at[0]
    )
    mine.start()
    my_bits = pltpu.make_async_copy(bits_ref, signs.at[spot], local_sem.at[1])
    my_bits.start()

    barrier = pltpu.get_barrier_semaphore()
    for k in range(1, SIDE):
        for p in (me ^ at(0, k, 0), me ^ at(0, 0, k), me ^ at(k, 0, 0)):
            pl.semaphore_signal(barrier, inc=1, device_id={"cols": p}, device_id_type=MESH)
    mirror = {"rows": my_row ^ 2, "cols": me ^ at(0, SIDE - 1, 0)}
    pl.semaphore_signal(barrier, inc=1, device_id=mirror, device_id_type=MESH)
    core = my_row % 2
    twin = {"rows": my_row ^ 1}

    @pl.when(core == 0)
    def _():
        pl.semaphore_signal(barrier, inc=1, device_id=twin, device_id_type=MESH)

    table[...] = sylvester(local, scale)
    peaks[...] = jnp.zeros_like(peaks)
    my_bits.wait()
    pl.semaphore_wait(barrier, 3 * (SIDE - 1) + 1 + core)

    @pl.when(core == 1)
    def _():
        pl.semaphore_signal(hello, inc=1, device_id=twin, device_id_type=MESH)


    def send_signs(step, first, size, peers):
        for p in peers:
            pltpu.make_async_remote_copy(
                src_ref=signs.at[pl.ds(first, size)], dst_ref=signs.at[pl.ds(first, size)],
                send_sem=sign_send.at[step], recv_sem=sign_recv.at[step],
                device_id={"cols": p}, device_id_type=MESH,
            ).start()

    def wait_signs(step, size, sem):
        wait_bytes(signs.at[pl.ds(0, (SIDE - 1) * size)], sem.at[step])

    def send_rows(c, p):
        pltpu.make_async_remote_copy(
            src_ref=w_ref.at[pl.ds(pl.multiple_of(p * total + starts[c], 8), chunks[c])],
            dst_ref=recv.at[me, pl.ds(starts[c], chunks[c])],
            send_sem=send_sem.at[c], recv_sem=recv_sem.at[c],
            device_id={"cols": p}, device_id_type=MESH,
        ).start()

    def send_chunk(c):
        def send(s, carry):
            send_rows(c, peer_of(s))
            return carry

        lax.fori_loop(SIDE, n, send, 0)

    others = range(1, SIDE)
    send_signs(0, spot, 1, [me ^ at(0, k, 0) for k in others])
    for c in range(count):
        for k in others:
            send_rows(c, me ^ at(0, k, 0))
    wait_signs(0, 1, sign_recv)
    send_signs(1, y * 16 + x * 4, 4, [me ^ at(0, 0, k) for k in others])
    wait_signs(1, 4, sign_recv)
    send_signs(2, y * 16, 16, [me ^ at(k, 0, 0) for k in others])
    wait_signs(2, 16, sign_recv)

    for c in range(min(AHEAD, count)):
        send_chunk(c)
    mine.wait()

    for c in range(count):
        if c + AHEAD < count:
            send_chunk(c + AHEAD)
        r, r0 = chunks[c], starts[c]
        wait_bytes(recv.at[pl.ds(0, n - 1), pl.ds(r0, r)], recv_sem.at[c])

        def inner(a, carry):
            xs = []
            for b in range(8):
                d = a * 8 + b
                place = (d // 16) * 16 + (d % 4) * 4 + (d // 4) % 4
                sign = (2 * signs[place] - 1).astype(jnp.float32)
                xs.append(recv[d, r0:r0 + r, :] * sign)
            for b, v in enumerate(butterfly(xs)):
                work[pl.ds(pl.multiple_of((a * 8 + b) * r, 8), r), :] = v
            return carry

        lax.fori_loop(0, n // 8, inner, 0)

        def outer(b, carry):
            where = [pl.ds(pl.multiple_of((a * 8 + b) * r, 8), r) for a in range(n // 8)]
            for w, v in zip(where, butterfly([work[w, :] for w in where])):
                work[w, :] = v
            return carry

        lax.fori_loop(0, 8, outer, 0)

        def product(m, carry):
            v = work[pl.ds(pl.multiple_of(m * TILE, TILE), TILE), :]
            high = v.astype(jnp.bfloat16)
            low = (v - high.astype(jnp.float32)).astype(jnp.bfloat16)
            result = jnp.dot(high, table[...], preferred_element_type=jnp.float32)
            result += jnp.dot(low, table[...], preferred_element_type=jnp.float32)
            for k in range(TILE // r):
                e = m * (TILE // r) + k
                block = result[k * r:(k + 1) * r, :]
                out_ref[r0:r0 + r, pl.ds(pl.multiple_of(e * local, local), local)] = block.astype(jnp.bfloat16)
                size = jnp.abs(block)
                top = size[0:8]
                for q in range(1, r // 8):
                    top = jnp.maximum(top, size[8 * q:8 * q + 8])
                if c < count - 1:
                    peaks[e] = jnp.maximum(peaks[e], top)
                else:
                    row_peaks[e] = jnp.maximum(row_peaks[e], jnp.max(top, axis=0, keepdims=True))
            return carry

        lax.fori_loop(0, n * r // TILE, product, 0)
        if c == count - 2:

            def shrink(i, carry):
                for k in range(8):
                    row_peaks[i * 8 + k] = jnp.max(peaks[i * 8 + k], axis=0, keepdims=True)
                return carry

            lax.fori_loop(0, n // 8, shrink, 0)

    half = my_row // 2

    def send_peak(p, row):
        pltpu.make_async_remote_copy(
            src_ref=row_peaks.at[p], dst_ref=peak_in.at[half * n + me],
            send_sem=peak_sem.at[0], recv_sem=peak_sem.at[1],
            device_id={"cols": p, "rows": row}, device_id_type=MESH,
        ).start()

    for away, k in ((2, 0), (0, 3), (2, 1), (2, 3), (0, 2), (2, 2), (0, 1), (0, 0)):

        def to_plane(t, carry):
            send_peak(me ^ at((t // 4) ^ 2, k, (t % 4) ^ 2), my_row ^ away)
            return carry

        if (away, k) != (0, 0):
            lax.fori_loop(0, SIDE * SIDE, to_plane, 0)
        else:
            for t in range(SIDE * SIDE):
                if t != 10:
                    to_plane(t, 0)
    top = row_peaks[me]
    wait_bytes(peak_in.at[pl.ds(0, 2 * n - 1)], peak_sem.at[1])
    peak_in[half * n + me] = top
    top = jnp.max(peak_in[...], axis=0)
    own[...] = top

    @pl.when(core == 0)
    def _():
        pl.semaphore_wait(hello, 1)

    pltpu.make_async_remote_copy(
        src_ref=own, dst_ref=core_in, send_sem=peak_sem.at[2], recv_sem=peak_sem.at[3],
        device_id=twin, device_id_type=MESH,
    ).start()
    wait_bytes(core_in, peak_sem.at[3])
    peak_ref[...] = jnp.maximum(top, core_in[...])

    wait_bytes(own, peak_sem.at[2])
    wait_bytes(peak_in.at[pl.ds(0, 2 * n - 1)], peak_sem.at[0])
    for step, size in enumerate((1, 4, 16)):
        wait_signs(step, size, sign_send)
    for c in range(count):
        wait_bytes(recv.at[pl.ds(0, n - 1), pl.ds(starts[c], chunks[c])], send_sem.at[c])


def body(weight, sign_bits):
    rows, local = weight.shape
    n, n_rows = lax.axis_size("cols"), lax.axis_size("rows")
    total, width = rows // n, local * n
    chunks = [BLOCK] * (total // BLOCK) + ([total % BLOCK] if total % BLOCK else [])
    out, peak = pl.pallas_call(
        functools.partial(kernel, n, n_rows, chunks, width ** -0.5),
        out_shape=(
            pltpu.VMEM((total, width), jnp.bfloat16),
            pltpu.VMEM((1, local), jnp.float32),
        ),
        in_specs=[pl.BlockSpec(memory_space=pl.ANY)] * 2,
        out_specs=[pl.BlockSpec(memory_space=pltpu.VMEM)] * 2,
        scratch_shapes=[
            pltpu.VMEM((n, total, local), jnp.float32),
            pltpu.VMEM((n, 1, local), jnp.int32),
            pltpu.VMEM((n * BLOCK, local), jnp.float32),
            pltpu.VMEM((local, local), jnp.bfloat16),
            pltpu.VMEM((n, 8, local), jnp.float32),
            pltpu.VMEM((n, 1, local), jnp.float32),
            pltpu.VMEM((2 * n, 1, local), jnp.float32),
            pltpu.VMEM((1, local), jnp.float32),
            pltpu.VMEM((1, local), jnp.float32),
            pltpu.SemaphoreType.DMA((len(chunks),)),
            pltpu.SemaphoreType.DMA((len(chunks),)),
            pltpu.SemaphoreType.DMA((2,)),
            pltpu.SemaphoreType.DMA((3,)),
            pltpu.SemaphoreType.DMA((3,)),
            pltpu.SemaphoreType.DMA((4,)),
            pltpu.SemaphoreType.REGULAR,
        ],
        compiler_params=pltpu.CompilerParams(collective_id=0, has_side_effects=True, vmem_limit_bytes=58 << 20),
        name="rotate",
    )(weight, sign_bits.reshape(1, local))
    return out, peak.reshape(local)


def solution(mesh):
    return jax.shard_map(
        body,
        mesh=mesh,
        in_specs=(P("rows", "cols"), P("cols")),
        out_specs=(P(("rows", "cols"), None), P("cols")),
        check_vma=False,
    )
```

time: 184 us -> 173 us (0.940)
  Pallas kernels: 179 us -> 170 us
  local copies, waits for them, and re-layouts: 4.5 us -> 2.32 us
    pallas_call x1, Pallas kernels: 179 us -> 170 us  [body(): pl.pallas_call(functools.partial(kernel, n, n_rows, chunks, width ** (-0....]
    unnamed x4 -> x2, local copies, waits for them, and re-layouts: 4.5 us -> 2.32 us
where the time goes in v2:
time: 173 us
  Pallas kernels  170 us (98%)
  local copies, waits for them, and re-layouts  2.32 us (1%)
    pallas_call x1, Pallas kernels, body(): pl.pallas_call(functools.partial(kernel, n, n_rows, chunks, width ** (-0....  170 us

profile of v2, /device:TPU:1, one launch (start us, length us, event | category | flops | bytes accessed | tf_op | source)
XLA Modules:
  0.0 172.7 jit_solution(10491180814944958030)
XLA Ops:
  0.6 169.8 %rotate.1 = (bf16[104,16384]{1,0:T(8,128)(2,1)S(1)}, f32[1,256]{1,0:T(1,128)S(1)}) custom-call(f32[6656,256]{1,0:T(8,128)} %w_ref.1, s32[1,256]{1,0:T(1,128)} %bitcast.3), custom_call_target="tpu_custom_call" | custom-call | tf_op jit(solution)/shard_map/rotate/pallas_call | solution.py:242
  170.4 1.8 %copy.6 = bf16[104,16384]{1,0:T(8,128)(2,1)} copy(bf16[104,16384]{1,0:T(8,128)(2,1)S(1)} %get-tuple-element.6) | data formatting | bytes 6815744
  172.1 0.6 copy.7

commit v3 on v2

--- a/solution.py
+++ b/solution.py
@@ -10,7 +10,8 @@
 MESH = pl.DeviceIdType.MESH
 BLOCK = 16
 TILE = 256
-AHEAD = 2
+PLANE = 3
+AHEAD = 7
 SIDE = 4
 
 
@@ -40,7 +41,7 @@
     n, n_rows, chunks, scale,
     w_ref, bits_ref, out_ref, peak_ref,
     recv, signs, work, table, peaks, row_peaks, peak_in, own, core_in,
-    send_sem, recv_sem, local_sem, sign_send, sign_recv, peak_sem, hello,
+    send_sem, recv_sem, local_sem, sign_send, sign_recv, peak_sem, hello, word,
 ):
     me = lax.axis_index("cols")
     my_row = lax.axis_index("rows")
@@ -67,28 +68,40 @@
     my_bits = pltpu.make_async_copy(bits_ref, signs.at[spot], local_sem.at[1])
     my_bits.start()
 
+    half, core = my_row // 2, my_row % 2
+    twin = {"rows": my_row ^ 1}
+    mirror = {"rows": my_row ^ 2, "cols": me ^ at(0, SIDE - 1, 0)}
+    others = range(1, SIDE)
+
+    def rank_z(v):
+        return jnp.where(half == 0, v, 2 * jnp.minimum(v, SIDE - 1 - v) + v // 2)
+
+    def rank(v):
+        return v ^ (v // 2)
+
+    line_z = [(me ^ at(0, k, 0), rank_z(z ^ k) < rank_z(z)) for k in others]
+    line_x = [(me ^ at(0, 0, k), rank(x ^ k) < rank(x)) for k in others]
+    line_y = [(me ^ at(k, 0, 0), rank(y ^ k) < rank(y)) for k in others]
+    pairs = [({"cols": p}, earlier, 0) for p, earlier in line_z]
+    pairs += [({"cols": p}, earlier, 1) for p, earlier in line_x + line_y]
+    pairs += [(mirror, half == 1, 2), (twin, core == 1, 2)]
+
+    def signal(sem, device):
+        pl.semaphore_signal(sem, inc=1, device_id=device, device_id_type=MESH)
+
+    def wait_some(sem, value):
+        @pl.when(value > 0)
+        def _():
+            pl.semaphore_wait(sem, value)
+
     barrier = pltpu.get_barrier_semaphore()
-    for k in range(1, SIDE):
-        for p in (me ^ at(0, k, 0), me ^ at(0, 0, k), me ^ at(k, 0, 0)):
-            pl.semaphore_signal(barrier, inc=1, device_id={"cols": p}, device_id_type=MESH)
-    mirror = {"rows": my_row ^ 2, "cols": me ^ at(0, SIDE - 1, 0)}
-    pl.semaphore_signal(barrier, inc=1, device_id=mirror, device_id_type=MESH)
-    core = my_row % 2
-    twin = {"rows": my_row ^ 1}
-
-    @pl.when(core == 0)
-    def _():
-        pl.semaphore_signal(barrier, inc=1, device_id=twin, device_id_type=MESH)
-
-    table[...] = sylvester(local, scale)
-    peaks[...] = jnp.zeros_like(peaks)
+    for device, earlier, _ in pairs:
+        pl.when(jnp.logical_not(earlier))(functools.partial(signal, barrier, device))
+    ahead_z, ahead_xy = rank_z(z), rank(x) + rank(y)
+    wait_some(barrier, ahead_z + ahead_xy + half + core)
+    for device, earlier, which in pairs:
+        pl.when(earlier)(functools.partial(signal, hello.at[which], device))
     my_bits.wait()
-    pl.semaphore_wait(barrier, 3 * (SIDE - 1) + 1 + core)
-
-    @pl.when(core == 1)
-    def _():
-        pl.semaphore_signal(hello, inc=1, device_id=twin, device_id_type=MESH)
-
 
     def send_signs(step, first, size, peers):
         for p in peers:
@@ -109,31 +122,43 @@
             device_id={"cols": p}, device_id_type=MESH,
         ).start()
 
-    def send_chunk(c):
+    def send_chunk(c, first, last):
         def send(s, carry):
             send_rows(c, peer_of(s))
             return carry
 
-        lax.fori_loop(SIDE, n, send, 0)
-
-    others = range(1, SIDE)
-    send_signs(0, spot, 1, [me ^ at(0, k, 0) for k in others])
-    for c in range(count):
-        for k in others:
-            send_rows(c, me ^ at(0, k, 0))
+        lax.fori_loop(first, last, send, 0)
+
+    plane = SIDE * SIDE
+
+    def along_z(p):
+        send_signs(0, spot, 1, [p])
+        for c in range(count):
+            send_rows(c, p)
+
+    for p, earlier in line_z:
+        pl.when(earlier)(functools.partial(along_z, p))
+    table[...] = sylvester(local, scale)
+    peaks[...] = jnp.zeros_like(peaks)
+    wait_some(hello.at[0], SIDE - 1 - ahead_z)
+    for p, earlier in line_z:
+        pl.when(jnp.logical_not(earlier))(functools.partial(along_z, p))
+    wait_some(hello.at[1], 2 * (SIDE - 1) - ahead_xy)
     wait_signs(0, 1, sign_recv)
-    send_signs(1, y * 16 + x * 4, 4, [me ^ at(0, 0, k) for k in others])
+    send_signs(1, y * 16 + x * 4, 4, [p for p, _ in line_x])
     wait_signs(1, 4, sign_recv)
-    send_signs(2, y * 16, 16, [me ^ at(k, 0, 0) for k in others])
+    send_signs(2, y * 16, 16, [p for p, _ in line_y])
+    for c in range(PLANE):
+        send_chunk(c, SIDE, plane)
     wait_signs(2, 16, sign_recv)
 
     for c in range(min(AHEAD, count)):
-        send_chunk(c)
+        send_chunk(c, plane if c < PLANE else SIDE, n)
     mine.wait()
 
     for c in range(count):
         if c + AHEAD < count:
-            send_chunk(c + AHEAD)
+            send_chunk(c + AHEAD, plane if c + AHEAD < PLANE else SIDE, n)
         r, r0 = chunks[c], starts[c]
         wait_bytes(recv.at[pl.ds(0, n - 1), pl.ds(r0, r)], recv_sem.at[c])
 
@@ -179,6 +204,14 @@
             return carry
 
         lax.fori_loop(0, n * r // TILE, product, 0)
+        if c == 1:
+            wait_some(hello.at[2], 2 - half - core)
+            for step, devices in enumerate((
+                [mirror, twin], *([{"cols": p} for p, _ in line] for line in (line_z, line_x, line_y)),
+            )):
+                for device in devices:
+                    signal(word.at[step], device)
+                pl.semaphore_wait(word.at[step], len(devices))
         if c == count - 2:
 
             def shrink(i, carry):
@@ -188,11 +221,10 @@
 
             lax.fori_loop(0, n // 8, shrink, 0)
 
-    half = my_row // 2
 
     def send_peak(p, row):
         pltpu.make_async_remote_copy(
-            src_ref=row_peaks.at[p], dst_ref=peak_in.at[half * n + me],
+            src_ref=row_peaks.at[p], dst_ref=peak_in.at[my_row * n + me],
             send_sem=peak_sem.at[0], recv_sem=peak_sem.at[1],
             device_id={"cols": p, "rows": row}, device_id_type=MESH,
         ).start()
@@ -200,7 +232,7 @@
     for away, k in ((2, 0), (0, 3), (2, 1), (2, 3), (0, 2), (2, 2), (0, 1), (0, 0)):
 
         def to_plane(t, carry):
-            send_peak(me ^ at((t // 4) ^ 2, k, (t % 4) ^ 2), my_row ^ away)
+            send_peak(me ^ at((t // 4) ^ 2, k, (t % 4) ^ 2), (half * 2) ^ away)
             return carry
 
         if (away, k) != (0, 0):
@@ -209,29 +241,46 @@
             for t in range(SIDE * SIDE):
                 if t != 10:
                     to_plane(t, 0)
-    top = row_peaks[me]
-    wait_bytes(peak_in.at[pl.ds(0, 2 * n - 1)], peak_sem.at[1])
-    peak_in[half * n + me] = top
-    top = jnp.max(peak_in[...], axis=0)
-    own[...] = top
+
+    @pl.when(core == 1)
+    def _():
+        send_peak(me, my_row ^ 1)
+        wait_bytes(core_in, peak_sem.at[3])
+        peak_ref[...] = core_in[...]
+        wait_bytes(row_peaks, peak_sem.at[0])
+        wait_bytes(row_peaks, peak_sem.at[0])
 
     @pl.when(core == 0)
     def _():
-        pl.semaphore_wait(hello, 1)
-
-    pltpu.make_async_remote_copy(
-        src_ref=own, dst_ref=core_in, send_sem=peak_sem.at[2], recv_sem=peak_sem.at[3],
-        device_id=twin, device_id_type=MESH,
-    ).start()
-    wait_bytes(core_in, peak_sem.at[3])
-    peak_ref[...] = jnp.maximum(top, core_in[...])
-
-    wait_bytes(own, peak_sem.at[2])
-    wait_bytes(peak_in.at[pl.ds(0, 2 * n - 1)], peak_sem.at[0])
+        top = row_peaks[me]
+        wait_bytes(peak_in.at[pl.ds(0, n_rows * n - 1)], peak_sem.at[1])
+        peak_in[my_row * n + me] = top
+        top = jnp.max(peak_in[...], axis=0)
+        own[...] = top
+        last = pltpu.make_async_remote_copy(
+            src_ref=own, dst_ref=core_in, send_sem=peak_sem.at[2], recv_sem=peak_sem.at[3],
+            device_id=twin, device_id_type=MESH,
+        )
+        last.start()
+        peak_ref[...] = top
+        wait_bytes(peak_in.at[pl.ds(0, 2 * n - 1)], peak_sem.at[0])
+        last.wait_send()
+
     for step, size in enumerate((1, 4, 16)):
         wait_signs(step, size, sign_send)
     for c in range(count):
         wait_bytes(recv.at[pl.ds(0, n - 1), pl.ds(starts[c], chunks[c])], send_sem.at[c])
+
+
+def store(out_ref, peak_ref, out_hbm, peak_hbm, sem):
+    rows = out_ref.shape[0]
+    copies = [(peak_ref, peak_hbm)]
+    copies += [(out_ref.at[pl.ds(i, 8)], out_hbm.at[pl.ds(i, 8)]) for i in range(0, rows, 8)]
+    copies = [pltpu.make_async_copy(a, b, sem.at[i]) for i, (a, b) in enumerate(copies)]
+    for copy in copies:
+        copy.start()
+    for copy in copies:
+        copy.wait()
 
 
 def body(weight, sign_bits):
@@ -254,7 +303,7 @@
             pltpu.VMEM((local, local), jnp.bfloat16),
             pltpu.VMEM((n, 8, local), jnp.float32),
             pltpu.VMEM((n, 1, local), jnp.float32),
-            pltpu.VMEM((2 * n, 1, local), jnp.float32),
+            pltpu.VMEM((n_rows * n, 1, local), jnp.float32),
             pltpu.VMEM((1, local), jnp.float32),
             pltpu.VMEM((1, local), jnp.float32),
             pltpu.SemaphoreType.DMA((len(chunks),)),
@@ -263,11 +312,24 @@
             pltpu.SemaphoreType.DMA((3,)),
             pltpu.SemaphoreType.DMA((3,)),
             pltpu.SemaphoreType.DMA((4,)),
-            pltpu.SemaphoreType.REGULAR,
+            pltpu.SemaphoreType.REGULAR((3,)),
+            pltpu.SemaphoreType.REGULAR((4,)),
         ],
         compiler_params=pltpu.CompilerParams(collective_id=0, has_side_effects=True, vmem_limit_bytes=58 << 20),
         name="rotate",
     )(weight, sign_bits.reshape(1, local))
+    out, peak = pl.pallas_call(
+        store,
+        out_shape=(
+            jax.ShapeDtypeStruct((total, width), jnp.bfloat16),
+            jax.ShapeDtypeStruct((1, local), jnp.float32),
+        ),
+        in_specs=[pl.BlockSpec(memory_space=pl.ANY)] * 2,
+        out_specs=[pl.BlockSpec(memory_space=pl.ANY)] * 2,
+        scratch_shapes=[pltpu.SemaphoreType.DMA((total // 8 + 1,))],
+        compiler_params=pltpu.CompilerParams(vmem_limit_bytes=1 << 20),
+        name="store",
+    )(out, peak)
     return out, peak.reshape(local)
 
 

time: 173 us -> 171 us (0.988)
  local copies, waits for them, and re-layouts: 2.32 us -> 0 us
    unnamed x2 -> x0, local copies, waits for them, and re-layouts: 2.32 us -> none
    pallas_call x0 -> x1, Pallas kernels: none -> 1.86 us  [body(): pl.pallas_call(store, out_shape=(jax.ShapeDtypeStruct((total, width), jnp...]
where the time goes in v3:
time: 171 us
  Pallas kernels  171 us (100%)
    pallas_call x1, Pallas kernels, body(): pl.pallas_call(functools.partial(kernel, n, n_rows, chunks, width ** (-0....  169 us

profile of v3, /device:TPU:1, one launch (start us, length us, event | category | flops | bytes accessed | tf_op | source)
XLA Modules:
  0.0 171.4 jit_solution(2039711996516636705)
XLA Ops:
  0.6 168.9 %rotate.1 = (bf16[104,16384]{1,0:T(8,128)(2,1)S(1)}, f32[1,256]{1,0:T(1,128)S(1)}) custom-call(f32[6656,256]{1,0:T(8,128)} %w_ref.1, s32[1,256]{1,0:T(1,128)} %bitcast.2), custom_call_target="tpu_custom_call" | custom-call | tf_op jit(solution)/shard_map/rotate/pallas_call | solution.py:291
  169.5 1.9 %store.1 = (bf16[104,16384]{1,0:T(8,128)(2,1)}, f32[1,256]{1,0:T(1,128)}) custom-call(bf16[104,16384]{1,0:T(8,128)(2,1)S(1)} %get-tuple-element.6.out_ref, f32[1,256]{1,0:T(1,128)S(1)} %get-tuple-element.7.peak_ref), custom_call_target="tpu_custom_call" | custom-call | tf_op jit(solution)/shard_map/store/pallas_call | solution.py:321

commit v4 on v3

--- a/solution.py
+++ b/solution.py
@@ -160,6 +160,7 @@
         if c + AHEAD < count:
             send_chunk(c + AHEAD, plane if c + AHEAD < PLANE else SIDE, n)
         r, r0 = chunks[c], starts[c]
+        tile = 512 if c == count - 1 else TILE
         wait_bytes(recv.at[pl.ds(0, n - 1), pl.ds(r0, r)], recv_sem.at[c])
 
         def inner(a, carry):
@@ -184,13 +185,13 @@
         lax.fori_loop(0, 8, outer, 0)
 
         def product(m, carry):
-            v = work[pl.ds(pl.multiple_of(m * TILE, TILE), TILE), :]
+            v = work[pl.ds(pl.multiple_of(m * tile, tile), tile), :]
             high = v.astype(jnp.bfloat16)
             low = (v - high.astype(jnp.float32)).astype(jnp.bfloat16)
             result = jnp.dot(high, table[...], preferred_element_type=jnp.float32)
             result += jnp.dot(low, table[...], preferred_element_type=jnp.float32)
-            for k in range(TILE // r):
-                e = m * (TILE // r) + k
+            for k in range(tile // r):
+                e = m * (tile // r) + k
                 block = result[k * r:(k + 1) * r, :]
                 out_ref[r0:r0 + r, pl.ds(pl.multiple_of(e * local, local), local)] = block.astype(jnp.bfloat16)
                 size = jnp.abs(block)
@@ -203,7 +204,7 @@
                     row_peaks[e] = jnp.maximum(row_peaks[e], jnp.max(top, axis=0, keepdims=True))
             return carry
 
-        lax.fori_loop(0, n * r // TILE, product, 0)
+        lax.fori_loop(0, n * r // tile, product, 0)
         if c == 1:
             wait_some(hello.at[2], 2 - half - core)
             for step, devices in enumerate((
@@ -229,7 +230,7 @@
             device_id={"cols": p, "rows": row}, device_id_type=MESH,
         ).start()
 
-    for away, k in ((2, 0), (0, 3), (2, 1), (2, 3), (0, 2), (2, 2), (0, 1), (0, 0)):
+    for away, k in ((2, 0), (2, 1), (2, 3), (2, 2), (0, 3), (0, 2), (0, 1), (0, 0)):
 
         def to_plane(t, carry):
             send_peak(me ^ at((t // 4) ^ 2, k, (t % 4) ^ 2), (half * 2) ^ away)

time: 171 us -> 171 us (level)
  no operation moved by 1% of the time
where the time goes in v4:
time: 171 us
  Pallas kernels  171 us (100%)
    pallas_call x1, Pallas kernels, body(): pl.pallas_call(functools.partial(kernel, n, n_rows, chunks, width ** (-0....  169 us

profile of v4, /device:TPU:1, one launch (start us, length us, event | category | flops | bytes accessed | tf_op | source)
XLA Modules:
  0.0 171.2 jit_solution(14714042632011896856)
XLA Ops:
  0.6 168.7 %rotate.1 = (bf16[104,16384]{1,0:T(8,128)(2,1)S(1)}, f32[1,256]{1,0:T(1,128)S(1)}) custom-call(f32[6656,256]{1,0:T(8,128)} %w_ref.1, s32[1,256]{1,0:T(1,128)} %bitcast.2), custom_call_target="tpu_custom_call" | custom-call | tf_op jit(solution)/shard_map/rotate/pallas_call | solution.py:292
  169.3 1.9 %store.1 = (bf16[104,16384]{1,0:T(8,128)(2,1)}, f32[1,256]{1,0:T(1,128)}) custom-call(bf16[104,16384]{1,0:T(8,128)(2,1)S(1)} %get-tuple-element.6.out_ref, f32[1,256]{1,0:T(1,128)S(1)} %get-tuple-element.7.peak_ref), custom_call_target="tpu_custom_call" | custom-call | tf_op jit(solution)/shard_map/store/pallas_call | solution.py:322
